TPU v7x, 128 devices: a whole 4x4x4 slice. The times are simulated.
128 devices in a mesh: store: 8 (over z, core), mp: 16 (over y, x).
Axes of the slice: x: 4, y: 4, z: 4, core: 2. Of those that a mesh axis runs over, the one named last changes fastest.
Arguments:
- tokens: bfloat16 [2048, 6144], P('store', 'mp'), may hold values from -6 to 6
- gain: float32 [6144], replicated, may hold values from 0.1 to 1.9
- base_projection_weight: bfloat16 [6144, 6144], P(None, 'mp'), may hold values from -0.078125 to 0.078125
- adapter_down_weight: bfloat16 [64, 64, 6144], P('store', None, 'mp'), may hold values from -0.078125 to 0.078125
- adapter_up_weight: bfloat16 [64, 64, 6144], P('store', None, 'mp'), may hold values from -0.75 to 0.75
- plan: int32 [8, 4], replicated, may hold values from 0 to 63, as said below
- target: int32 [2048, 1], P('store'), may hold values from 0 to 7; in each aligned block of 256 rows (0 to 255, 256 to 511, ...) at most 64 rows name the same one
- slot: int32 [2048], P('store'), may hold values from 0 to 11
Outputs:
- hidden_out: bfloat16 [2048, 6144], P('store', 'mp')
Inputs may be any that keep to these rules, and one draw needn't show every extreme that they name: plan[g, r] is an adapter owned by a store group other than g; adapter a is owned by group a // 8. `target`: among the 256 rows of one store group at most 64 name the same group, a bound that some block reaches.
All inputs are finite; a program needn't handle non-finite values.
Results may differ from a plain program's by a relative error of at most 0.0063.
Values may be sent and summed in bfloat16 or wider, within the bound.
A program may use at most 64 MiB of HBM per device.

v0:
```python
import jax
import jax.numpy as jnp
from jax import lax
from jax.sharding import PartitionSpec as P

STEPS = 4
CAP = 64
adapter_scale = 0.5


def local(
    tokens, gain, base_projection_weight, adapter_down_weight, adapter_up_weight, plan, target, slot
):
    store_count = lax.axis_size("store")
    group = lax.axis_index("store")
    owned_adapters = adapter_down_weight.shape[0]
    rank_position = adapter_down_weight.shape[1]
    width_portion = adapter_down_weight.shape[2]
    replica_count = plan.shape[1]
    n_slots = owned_adapters + replica_count
    flattened_down = adapter_down_weight.reshape(owned_adapters, rank_position * width_portion)
    flattened_up = adapter_up_weight.reshape(owned_adapters, rank_position * width_portion)
    own_plan = lax.dynamic_slice_in_dim(plan, group, 1, 0)[0]
    pieces = (
        lax.all_gather(flattened_down, "store", axis=0, tiled=True),
        lax.all_gather(flattened_up, "store", axis=0, tiled=True),
    )
    count = pieces[0].shape[0]
    select = (own_plan[:, None] == jnp.arange(count, dtype=jnp.int32)[None, :]).astype(jnp.bfloat16)
    replica_down_factor = jnp.dot(select, pieces[0], preferred_element_type=jnp.float32)
    replica_up_factor = jnp.dot(select, pieces[1], preferred_element_type=jnp.float32)
    host_down = jnp.concatenate(
        [
            adapter_down_weight,
            replica_down_factor.astype(jnp.bfloat16).reshape(
                replica_count, rank_position, width_portion
            ),
        ],
        0,
    )
    host_down = host_down.reshape(n_slots * rank_position, width_portion)
    host_up = jnp.concatenate(
        [
            adapter_up_weight,
            replica_up_factor.astype(jnp.bfloat16).reshape(
                replica_count, rank_position, width_portion
            ),
        ],
        0,
    )
    host_up = host_up.reshape(n_slots * rank_position, width_portion)
    target_group = target[:, 0]
    member = (target_group[:, None] == jnp.arange(store_count, dtype=jnp.int32)[None, :]).astype(
        jnp.int32
    )
    earlier = jnp.cumsum(member, axis=0) - member
    bucket_place = jnp.sum(earlier * member, axis=1)
    row_index = target_group * CAP + bucket_place
    slot_buffer = (
        jnp.full((store_count * CAP,), -1, jnp.int32)
        .at[row_index]
        .set(slot)
        .reshape(store_count, CAP)
    )
    state = tokens
    column_start = lax.axis_index("mp") * width_portion
    for step in range(STEPS):
        whole = lax.all_gather(state, "mp", axis=1, tiled=True)
        values = whole.astype(jnp.float32)
        mean_sq = jnp.mean(values * values, axis=1, keepdims=True)
        normed = (values * lax.rsqrt(mean_sq + 1e-05) * gain[None, :]).astype(jnp.bfloat16)
        mine = lax.dynamic_slice_in_dim(normed, column_start, width_portion, 1)
        row_buffer = (
            jnp.zeros((store_count * CAP, width_portion), jnp.bfloat16).at[row_index].set(mine)
        )
        row_buffer = row_buffer.reshape(store_count, CAP, width_portion)
        rows = lax.all_to_all(row_buffer, "store", split_axis=0, concat_axis=0, tiled=True)
        slots_in = lax.all_to_all(slot_buffer, "store", split_axis=0, concat_axis=0, tiled=True)
        senders, adapter_count = slots_in.shape
        total_rows = senders * adapter_count
        flat_rows = rows.reshape(total_rows, width_portion)
        partial_value = lax.dot_general(
            flat_rows, host_down, (((1,), (1,)), ((), ())), preferred_element_type=jnp.float32
        )
        selected_adapter = (
            slots_in.reshape(total_rows)[:, None] == jnp.arange(n_slots, dtype=jnp.int32)[None, :]
        )
        partial_value = jnp.sum(
            partial_value.reshape(total_rows, n_slots, rank_position)
            * selected_adapter[:, :, None].astype(jnp.float32),
            axis=1,
        )
        summed_share = lax.psum_scatter(
            partial_value, "mp", scatter_dimension=0, tiled=True
        ).astype(jnp.bfloat16)
        inner = lax.all_gather(summed_share, "mp", axis=0, tiled=True)
        spread_rows = (
            selected_adapter[:, :, None].astype(jnp.bfloat16) * inner[:, None, :]
        ).reshape(total_rows, n_slots * rank_position)
        outer = jnp.dot(spread_rows, host_up, preferred_element_type=jnp.float32)
        outer = (
            (adapter_scale * outer)
            .astype(jnp.bfloat16)
            .reshape(senders, adapter_count, width_portion)
        )
        returned = lax.all_to_all(outer, "store", split_axis=0, concat_axis=0, tiled=True)
        delta = returned.reshape(store_count * CAP, width_portion)[row_index]
        base = jnp.dot(normed, base_projection_weight, preferred_element_type=jnp.float32)
        state = (state.astype(jnp.float32) + base + delta.astype(jnp.float32)).astype(jnp.bfloat16)
    return state


def solution(mesh):
    return jax.shard_map(
        local,
        mesh=mesh,
        in_specs=(
            P("store", "mp"),
            P(),
            P(None, "mp"),
            P("store", None, "mp"),
            P("store", None, "mp"),
            P(),
            P("store", None),
            P("store"),
        ),
        out_specs=P("store", "mp"),
        check_vma=False,
    )
```

profile of v0, /device:TPU:1, one launch (start us, length us, event | category | flops | bytes accessed | tf_op | source)
XLA Modules:
  0.0 813.4 jit_solution(17470650637500841050)
XLA Ops:
  7.3 2.0 copy.35
  9.4 2.0 copy.37
  16.6 6.8 all-to-all-start
  23.4 1.8 constant_dynamic-update-slice_fusion
  26.2 1.9 all-to-all-done
  29.9 33.1 %all-gather.7.cloned.1.call-done = bf16[256,6144]{1,0:T(8,128)(2,1)} async-done(((bf16[256,384]{1,0:T(8,128)(2,1)}), bf16[256,6144]{1,0:T(8,128)(2,1)}) %all-gather.7.cloned.1.call-update) | async-done | bytes 3145744 | tf_op jit(solution)/shard_map/all_gather | solution.py:68
  63.0 2.7 fusion
  65.8 1.8 fusion.2
  67.7 2.3 scatter_custom_fusion.1
  69.9 6.5 all-to-all-start.1
  76.4 21.6 %all-gather.9.cloned.1.call-done = bf16[64,24576]{1,0:T(8,128)(2,1)} async-done(((bf16[8,24576]{1,0:T(8,128)(2,1)}), bf16[64,24576]{1,0:T(8,128)(2,1)}) %all-gather.9.cloned.1.call-update) | async-done | bytes 3145744 | tf_op jit(solution)/shard_map/all_gather | solution.py:25
  98.0 2.5 convolution_convert_fusion.1
  101.2 2.3 multiply_reduce_fusion.3
  103.5 1.8 copy.27
  105.3 20.9 %all-gather.11.cloned.1.call-done = bf16[64,24576]{1,0:T(8,128)(2,1)} async-done(((bf16[8,24576]{1,0:T(8,128)(2,1)}), bf16[64,24576]{1,0:T(8,128)(2,1)}) %all-gather.11.cloned.1.call-update) | async-done | bytes 3145744 | tf_op jit(solution)/shard_map/all_gather | solution.py:26
  126.2 2.5 convolution_convert_fusion
  129.4 70.7 %reduce-scatter.13.cloned.1.call-done = f32[32,64]{1,0:T(8,128)} async-done(((f32[512,64]{1,0:T(8,128)}), f32[32,64]{1,0:T(8,128)}) %reduce-scatter.13.cloned.1.call-update) | async-done | bytes 8208 | tf_op jit(solution)/shard_map/reduce_scatter | solution.py:93
  200.9 17.0 %all_gather.32 = bf16[512,64]{1,0:T(8,128)(2,1)S(1)} all-gather(bf16[32,64]{1,0:T(8,128)(2,1)S(1)} %convert_element_type.128), channel_id=1, replica_groups=mesh['store'=8,'mp'=16] {'mp'}, dimensions={0}, use_global_device_ids=true | all-gather | bytes 69632 | tf_op jit(solution)/shard_map/all_gather | solution.py:96
  217.9 2.4 fusion.16
  220.4 12.9 %all-to-all-start.2 = ((bf16[8,64,384]{2,1,0:T(8,128)(2,1)}), bf16[8,64,384]{2,1,0:T(8,128)(2,1)S(1)}, u32[]{:S(2)}, u32[]{:S(2)}) async-start(bf16[8,64,384]{2,1,0:T(8,128)(2,1)} %bitcast.115), calls=%async_computation.2 | async-start | bytes 786432 | tf_op jit(solution)/shard_map/all_to_all | solution.py:106
  233.2 7.7 all-to-all-done.2
  240.9 1.8 gather_fusion
  242.8 5.0 fusion.27
  248.0 47.6 %all-gather.13.cloned.1.call-done = bf16[256,6144]{1,0:T(8,128)(2,1)} async-done(((bf16[256,384]{1,0:T(8,128)(2,1)}), bf16[256,6144]{1,0:T(8,128)(2,1)}) %all-gather.13.cloned.1.call-update) | async-done | bytes 3145744 | tf_op jit(solution)/shard_map/all_gather | solution.py:68
  295.6 2.7 fusion.3
  301.2 14.3 %all_to_all.52 = bf16[8,64,384]{2,1,0:T(8,128)(2,1)S(1)} all-to-all(bf16[8,64,384]{2,1,0:T(8,128)(2,1)S(1)} %bitcast.110), channel_id=1, replica_groups=mesh['store'=8,'mp'=16] {'store'}, dimensions={0} | all-to-all | bytes 786432 | tf_op jit(solution)/shard_map/all_to_all | solution.py:77
  318.1 69.2 %reduce-scatter.15.cloned.1.call-done = f32[32,64]{1,0:T(8,128)} async-done(((f32[512,64]{1,0:T(8,128)}), f32[32,64]{1,0:T(8,128)}) %reduce-scatter.15.cloned.1.call-update) | async-done | bytes 8208 | tf_op jit(solution)/shard_map/reduce_scatter | solution.py:93
  388.0 17.0 %all_gather.35 = bf16[512,64]{1,0:T(8,128)(2,1)S(1)} all-gather(bf16[32,64]{1,0:T(8,128)(2,1)S(1)} %convert_element_type.136), channel_id=1, replica_groups=mesh['store'=8,'mp'=16] {'mp'}, dimensions={0}, use_global_device_ids=true | all-gather | bytes 69632 | tf_op jit(solution)/shard_map/all_gather | solution.py:96
  406.7 20.7 %all_to_all.53 = bf16[8,64,384]{2,1,0:T(8,128)(2,1)S(1)} all-to-all(bf16[8,64,384]{2,1,0:T(8,128)(2,1)S(1)} %bitcast.119), channel_id=1, replica_groups=mesh['store'=8,'mp'=16] {'store'}, dimensions={0} | all-to-all | bytes 786432 | tf_op jit(solution)/shard_map/all_to_all | solution.py:106
  427.4 1.8 gather_fusion.1
  429.3 5.0 fusion.26
  434.4 47.4 %all-gather.15.cloned.1.call-done = bf16[256,6144]{1,0:T(8,128)(2,1)} async-done(((bf16[256,384]{1,0:T(8,128)(2,1)}), bf16[256,6144]{1,0:T(8,128)(2,1)}) %all-gather.15.cloned.1.call-update) | async-done | bytes 3145744 | tf_op jit(solution)/shard_map/all_gather | solution.py:68
  481.8 2.7 fusion.6
  487.3 14.3 %all_to_all.54 = bf16[8,64,384]{2,1,0:T(8,128)(2,1)S(1)} all-to-all(bf16[8,64,384]{2,1,0:T(8,128)(2,1)S(1)} %bitcast.111), channel_id=1, replica_groups=mesh['store'=8,'mp'=16] {'store'}, dimensions={0} | all-to-all | bytes 786432 | tf_op jit(solution)/shard_map/all_to_all | solution.py:77
  501.6 1.7 multiply_reduce_fusion.1
  504.2 69.2 %reduce-scatter.17.cloned.1.call-done = f32[32,64]{1,0:T(8,128)} async-done(((f32[512,64]{1,0:T(8,128)}), f32[32,64]{1,0:T(8,128)}) %reduce-scatter.17.cloned.1.call-update) | async-done | bytes 8208 | tf_op jit(solution)/shard_map/reduce_scatter | solution.py:93
  574.1 17.0 %all_gather.37 = bf16[512,64]{1,0:T(8,128)(2,1)S(1)} all-gather(bf16[32,64]{1,0:T(8,128)(2,1)S(1)} %convert_element_type.143), channel_id=1, replica_groups=mesh['store'=8,'mp'=16] {'mp'}, dimensions={0}, use_global_device_ids=true | all-gather | bytes 69632 | tf_op jit(solution)/shard_map/all_gather | solution.py:96
  592.9 20.7 %all_to_all.55 = bf16[8,64,384]{2,1,0:T(8,128)(2,1)S(1)} all-to-all(bf16[8,64,384]{2,1,0:T(8,128)(2,1)S(1)} %bitcast.121), channel_id=1, replica_groups=mesh['store'=8,'mp'=16] {'store'}, dimensions={0} | all-to-all | bytes 786432 | tf_op jit(solution)/shard_map/all_to_all | solution.py:106
  613.6 1.8 gather_fusion.2
  615.4 5.0 fusion.25
  620.5 47.4 %all-gather.17.cloned.1.call-done = bf16[256,6144]{1,0:T(8,128)(2,1)} async-done(((bf16[256,384]{1,0:T(8,128)(2,1)}), bf16[256,6144]{1,0:T(8,128)(2,1)}) %all-gather.17.cloned.1.call-update) | async-done | bytes 3145744 | tf_op jit(solution)/shard_map/all_gather | solution.py:68
  667.9 2.7 fusion.9
  673.5 14.3 %all_to_all.56 = bf16[8,64,384]{2,1,0:T(8,128)(2,1)S(1)} all-to-all(bf16[8,64,384]{2,1,0:T(8,128)(2,1)S(1)} %bitcast.109), channel_id=1, replica_groups=mesh['store'=8,'mp'=16] {'store'}, dimensions={0} | all-to-all | bytes 786432 | tf_op jit(solution)/shard_map/all_to_all | solution.py:77
  690.3 69.2 %reduce-scatter.19.cloned.1.call-done = f32[32,64]{1,0:T(8,128)} async-done(((f32[512,64]{1,0:T(8,128)}), f32[32,64]{1,0:T(8,128)}) %reduce-scatter.19.cloned.1.call-update) | async-done | bytes 8208 | tf_op jit(solution)/shard_map/reduce_scatter | solution.py:93
  760.2 17.0 %all_gather.39 = bf16[512,64]{1,0:T(8,128)(2,1)S(1)} all-gather(bf16[32,64]{1,0:T(8,128)(2,1)S(1)} %convert_element_type.150), channel_id=1, replica_groups=mesh['store'=8,'mp'=16] {'mp'}, dimensions={0}, use_global_device_ids=true | all-gather | bytes 69632 | tf_op jit(solution)/shard_map/all_gather | solution.py:96
  779.0 20.7 %all_to_all.57 = bf16[8,64,384]{2,1,0:T(8,128)(2,1)S(1)} all-to-all(bf16[8,64,384]{2,1,0:T(8,128)(2,1)S(1)} %bitcast.117), channel_id=1, replica_groups=mesh['store'=8,'mp'=16] {'store'}, dimensions={0} | all-to-all | bytes 786432 | tf_op jit(solution)/shard_map/all_to_all | solution.py:106
  799.7 1.8 gather_fusion.3
  801.5 5.0 fusion.24
  (91 shorter events, 33.4 us)
Async XLA Ops:
  6.5 19.4 %copy-start = (s32[8,4]{0,1:T(4,128)S(1)}, s32[8,4]{0,1:T(4,128)}, u32[]{:S(2)}) copy-start(s32[8,4]{0,1:T(4,128)} %param.13) | copy-start | bytes 388
  6.5 18.6 %copy-start.5 = (bf16[8,64,384]{2,1,0:T(8,128)(2,1)S(1)}, bf16[8,64,384]{2,1,0:T(8,128)(2,1)}, u32[]{:S(2)}) copy-start(bf16[8,64,384]{2,1,0:T(8,128)(2,1)} %param.12) | copy-start | bytes 1179652
  6.5 56.5 %all-gather.7.cloned.1.call-start = ((), (), s32[]{:S(2)}) async-start(), calls=%async_computation.13 | async-start | bytes 3342336 | tf_op jit(solution)/shard_map/all_gather | solution.py:68
  7.3 90.7 %all-gather.9.cloned.1.call-start = ((), (), s32[]{:S(2)}) async-start(), calls=%async_computation.14 | async-start | bytes 3538944 | tf_op jit(solution)/shard_map/all_gather | solution.py:25
  9.3 116.9 %all-gather.11.cloned.1.call-start = ((), (), s32[]{:S(2)}) async-start(), calls=%async_computation.15 | async-start | bytes 3538944 | tf_op jit(solution)/shard_map/all_gather | solution.py:26
  16.6 11.4 %all-to-all-start = ((s32[8,1,64]{2,1,0:T(1,128)}), s32[8,1,64]{2,1,0:T(1,128)S(1)}, u32[]{:S(2)}, u32[]{:S(2)}) async-start(s32[8,1,64]{2,1,0:T(1,128)} %all_to_all.33), calls=%async_computation | async-start | bytes 8192 | tf_op jit(solution)/shard_map/all_to_all | solution.py:78
  63.0 2.8 copy-start.1
  69.9 31.3 %all-to-all-start.1 = ((bf16[8,64,384]{2,1,0:T(8,128)(2,1)}), bf16[8,64,384]{2,1,0:T(8,128)(2,1)S(1)}, u32[]{:S(2)}, u32[]{:S(2)}) async-start(bf16[8,64,384]{2,1,0:T(8,128)(2,1)} %bitcast.6), calls=%async_computation.1 | async-start | bytes 786432 | tf_op jit(solution)/shard_map/all_to_all | solution.py:77
  76.4 123.8 %reduce-scatter.13.cloned.1.call-start = ((), (), s32[]{:S(2)}) async-start(), calls=%async_computation.19 | async-start | bytes 278528 | tf_op jit(solution)/shard_map/reduce_scatter | solution.py:93
  103.5 114.4 %copy-start.9 = (bf16[512,12]{0,1:T(8,128)(2,1)S(1)}, bf16[512,12]{0,1:T(8,128)(2,1)}, u32[]{:S(2)}) copy-start(bf16[512,12]{0,1:T(8,128)(2,1)} %get-tuple-element.5) | copy-start | bytes 36868
  220.4 20.6 %all-to-all-start.2 = ((bf16[8,64,384]{2,1,0:T(8,128)(2,1)}), bf16[8,64,384]{2,1,0:T(8,128)(2,1)S(1)}, u32[]{:S(2)}, u32[]{:S(2)}) async-start(bf16[8,64,384]{2,1,0:T(8,128)(2,1)} %bitcast.115), calls=%async_computation.2 | async-start | bytes 786432 | tf_op jit(solution)/shard_map/all_to_all | solution.py:106
  233.2 62.4 %all-gather.13.cloned.1.call-start = ((), (), s32[]{:S(2)}) async-start(), calls=%async_computation.16 | async-start | bytes 3342336 | tf_op jit(solution)/shard_map/all_gather | solution.py:68
  247.8 50.6 %copy-start.6 = (f32[6144]{0:T(1024)S(1)}, f32[6144]{0:T(1024)}, u32[]{:S(2)}) copy-start(f32[6144]{0:T(1024)} %param.9) | copy-start | bytes 73732
  247.8 139.4 %reduce-scatter.15.cloned.1.call-start = ((), (), s32[]{:S(2)}) async-start(), calls=%async_computation.20 | async-start | bytes 278528 | tf_op jit(solution)/shard_map/reduce_scatter | solution.py:93
  295.6 2.8 copy-start.2
  315.5 89.5 %copy-start.10 = (bf16[512,12]{0,1:T(8,128)(2,1)S(1)}, bf16[512,12]{0,1:T(8,128)(2,1)}, u32[]{:S(2)}) copy-start(bf16[512,12]{0,1:T(8,128)(2,1)} %get-tuple-element.5) | copy-start | bytes 36868
  318.0 163.8 %all-gather.15.cloned.1.call-start = ((), (), s32[]{:S(2)}) async-start(), calls=%async_computation.17 | async-start | bytes 3342336 | tf_op jit(solution)/shard_map/all_gather | solution.py:68
  434.3 50.3 %copy-start.7 = (f32[6144]{0:T(1024)S(1)}, f32[6144]{0:T(1024)}, u32[]{:S(2)}) copy-start(f32[6144]{0:T(1024)} %param.9) | copy-start | bytes 73732
  434.3 139.1 %reduce-scatter.17.cloned.1.call-start = ((), (), s32[]{:S(2)}) async-start(), calls=%async_computation.21 | async-start | bytes 278528 | tf_op jit(solution)/shard_map/reduce_scatter | solution.py:93
  481.8 2.8 copy-start.3
  501.6 89.5 %copy-start.11 = (bf16[512,12]{0,1:T(8,128)(2,1)S(1)}, bf16[512,12]{0,1:T(8,128)(2,1)}, u32[]{:S(2)}) copy-start(bf16[512,12]{0,1:T(8,128)(2,1)} %get-tuple-element.5) | copy-start | bytes 36868
  504.2 163.8 %all-gather.17.cloned.1.call-start = ((), (), s32[]{:S(2)}) async-start(), calls=%async_computation.18 | async-start | bytes 3342336 | tf_op jit(solution)/shard_map/all_gather | solution.py:68
  620.4 50.3 %copy-start.8 = (f32[6144]{0:T(1024)S(1)}, f32[6144]{0:T(1024)}, u32[]{:S(2)}) copy-start(f32[6144]{0:T(1024)} %param.9) | copy-start | bytes 73732
  620.4 139.1 %reduce-scatter.19.cloned.1.call-start = ((), (), s32[]{:S(2)}) async-start(), calls=%async_computation.22 | async-start | bytes 278528 | tf_op jit(solution)/shard_map/reduce_scatter | solution.py:93
  667.9 2.8 copy-start.4
  687.8 89.5 %copy-start.12 = (bf16[512,12]{0,1:T(8,128)(2,1)S(1)}, bf16[512,12]{0,1:T(8,128)(2,1)}, u32[]{:S(2)}) copy-start(bf16[512,12]{0,1:T(8,128)(2,1)} %get-tuple-element.5) | copy-start | bytes 36868
Sparse Core Ops, SparseCore 0:
  9.4 53.5 all-gather.6
  64.7 33.2 all-gather.8
  99.7 26.5 all-gather.10
  129.3 70.8 reduce-scatter.12
  247.9 47.6 all-gather.12
  318.1 69.0 reduce-scatter.14
  434.4 47.3 all-gather.14
  504.3 69.0 reduce-scatter.16
  620.6 47.3 all-gather.16
  690.4 69.0 reduce-scatter.18
where the time goes:
time: 815 us; the launch traced here: 813 us
  waiting for transfers between devices  507 us (62%)
  blocking collectives  173 us (21%)
  matrix products  39.8 us (5%)
  local copies, waits for them, and re-layouts  30.5 us (4%)
  starting transfers between devices  26.6 us (3%)
  other arithmetic  23 us (3%)
  between operations  13.8 us (2%)
    reduce_scatter x4, waiting for transfers between devices, local(): lax.psum_scatter(partial_value, 'mp', scatter_dimension=0, tiled=True)  278 us
    all_gather x4, waiting for transfers between devices, local(): whole = lax.all_gather(state, 'mp', axis=1, tiled=True)  176 us
    all_gather x4, blocking collectives, local(): inner = lax.all_gather(summed_share, 'mp', axis=0, tiled=True)  67.8 us
    all_to_all x3, blocking collectives, local(): lax.all_to_all(outer, 'store', split_axis=0, concat_axis=0, tiled=True)  62.2 us
    all_to_all x3, blocking collectives, local(): lax.all_to_all(row_buffer, 'store', split_axis=0, concat_axis=0, tiled=True)  42.9 us
    all_gather x1, waiting for transfers between devices, local(): lax.all_gather(flattened_down, 'store', axis=0, tiled=True)  21.6 us
    all_gather x1, waiting for transfers between devices, local(): lax.all_gather(flattened_up, 'store', axis=0, tiled=True)  20.9 us
    dot_general x4, matrix products, local(): jnp.dot(normed, base_projection_weight, preferred_element_type=jnp.float32)  20.1 us
  transfers between devices with their start and end apart: 13, of which 12 were waited for; matrix products, arithmetic and copies ran while one was open for 4% of the time, Pallas kernels for 0%

commit v1 on v0

--- a/solution.py
+++ b/solution.py
@@ -65,7 +65,16 @@
     state = tokens
     column_start = lax.axis_index("mp") * width_portion
     for step in range(STEPS):
-        whole = lax.all_gather(state, "mp", axis=1, tiled=True)
+        ways = lax.axis_size("mp")
+        up = [(d, (d + 1) % ways) for d in range(ways)]
+        down = [(d, (d - 1) % ways) for d in range(ways)]
+        earlier_2, later = ([state], [state])
+        for _ in range(ways // 2):
+            earlier_2.append(lax.ppermute(earlier_2[-1], "mp", up))
+        for _ in range((ways - 1) // 2):
+            later.append(lax.ppermute(later[-1], "mp", down))
+        line = jnp.concatenate([*earlier_2[::-1], *later[1:]], axis=1)
+        whole = jnp.roll(line, (lax.axis_index("mp") - ways // 2) * state.shape[1], axis=1)
         values = whole.astype(jnp.float32)
         mean_sq = jnp.mean(values * values, axis=1, keepdims=True)
         normed = (values * lax.rsqrt(mean_sq + 1e-05) * gain[None, :]).astype(jnp.bfloat16)

time: 815 us -> 901 us (1.11)
  starting transfers between devices: 26.6 us -> 173 us
  waiting for transfers between devices: 507 us -> 412 us
  blocking collectives: 173 us -> 191 us
  other arithmetic: 23 us -> 33.3 us
    all_gather x4 -> x0, waiting for transfers between devices: 176 us -> none  [local(): whole = lax.all_gather(state, 'mp', axis=1, tiled=True)]
    ppermute x0 -> x60, starting transfers between devices: none -> 142 us  [the longest x28 139 us: local(): later.append(lax.ppermute(later[-1], 'mp', down))]
    ppermute x0 -> x60, waiting for transfers between devices: none -> 119 us  [the longest x32 113 us: local(): earlier_2.append(lax.ppermute(earlier_2[-1], 'mp', up))]
    all_gather x1, waiting for transfers between devices: 21.6 us -> 0.01 us  [local(): lax.all_gather(flattened_down, 'store', axis=0, tiled=True)]
    all_gather x1, waiting for transfers between devices: 20.9 us -> 0.02 us  [local(): lax.all_gather(flattened_up, 'store', axis=0, tiled=True)]
    all_to_all x3, blocking collectives: 42.9 us -> 60.1 us  [local(): lax.all_to_all(row_buffer, 'store', split_axis=0, concat_axis=0, tiled=True)]
  transfers between devices with their start and end apart: 13 -> 69, of which waited for: 12 -> 41; matrix products, arithmetic and copies ran while one was open for 4% -> 4% of each run, Pallas kernels for 0% -> 0%
where the time goes in v1:
time: 901 us; the launch traced here: 894 us
  waiting for transfers between devices  412 us (46%)
  blocking collectives  191 us (21%)
  starting transfers between devices  173 us (19%)
  matrix products  37.8 us (4%)
  other arithmetic  33.3 us (4%)
  local copies, waits for them, and re-layouts  32.8 us (4%)
  between operations  14.7 us (2%)
    reduce_scatter x4, waiting for transfers between devices, local(): lax.psum_scatter(partial_value, 'mp', scatter_dimension=0, tiled=True)  280 us
    ppermute x28, starting transfers between devices, local(): later.append(lax.ppermute(later[-1], 'mp', down))  139 us
    ppermute x32, waiting for transfers between devices, local(): earlier_2.append(lax.ppermute(earlier_2[-1], 'mp', up))  113 us
    all_gather x4, blocking collectives, local(): inner = lax.all_gather(summed_share, 'mp', axis=0, tiled=True)  68.3 us
    all_to_all x3, blocking collectives, local(): lax.all_to_all(outer, 'store', split_axis=0, concat_axis=0, tiled=True)  62.9 us
    all_to_all x3, blocking collectives, local(): lax.all_to_all(row_buffer, 'store', split_axis=0, concat_axis=0, tiled=True)  60.1 us
  transfers between devices with their start and end apart: 69, of which 41 were waited for; matrix products, arithmetic and copies ran while one was open for 4% of the time, Pallas kernels for 0%

profile of v1, /device:TPU:1, one launch (start us, length us, event | category | flops | bytes accessed | tf_op | source)
XLA Modules:
  0.0 894.0 jit_solution(4918630844477938503)
XLA Ops:
  10.8 8.5 collective-permute-done
  29.9 4.9 collective-permute-start.9
  37.4 5.2 collective-permute-start.10
  45.2 5.2 collective-permute-start.11
  54.3 10.8 %all-to-all-start = ((s32[8,1,64]{2,1,0:T(1,128)}), s32[8,1,64]{2,1,0:T(1,128)S(1)}, u32[]{:S(2)}, u32[]{:S(2)}) async-start(s32[8,1,64]{2,1,0:T(1,128)} %all_to_all.33), calls=%async_computation | async-start | bytes 8192 | tf_op jit(solution)/shard_map/all_to_all | solution.py:87
  65.0 5.1 collective-permute-start.12
  74.3 5.5 collective-permute-start.13
  83.1 5.7 collective-permute-start.14
  100.4 6.7 all-to-all-start.1
  122.1 68.2 %reduce-scatter.13.cloned.1.call-done = f32[32,64]{1,0:T(8,128)} async-done(((f32[512,64]{1,0:T(8,128)}), f32[32,64]{1,0:T(8,128)}) %reduce-scatter.13.cloned.1.call-update) | async-done | bytes 8208 | tf_op jit(solution)/shard_map/reduce_scatter | solution.py:102
  191.1 17.2 %all_gather.19 = bf16[512,64]{1,0:T(8,128)(2,1)S(1)} all-gather(bf16[32,64]{1,0:T(8,128)(2,1)S(1)} %convert_element_type.128), channel_id=1, replica_groups=mesh['store'=8,'mp'=16] {'mp'}, dimensions={0}, use_global_device_ids=true | all-gather | bytes 69632 | tf_op jit(solution)/shard_map/all_gather | solution.py:105
  210.8 12.9 %all-to-all-start.2 = ((bf16[8,64,384]{2,1,0:T(8,128)(2,1)}), bf16[8,64,384]{2,1,0:T(8,128)(2,1)S(1)}, u32[]{:S(2)}, u32[]{:S(2)}) async-start(bf16[8,64,384]{2,1,0:T(8,128)(2,1)} %bitcast.110), calls=%async_computation.2 | async-start | bytes 786432 | tf_op jit(solution)/shard_map/all_to_all | solution.py:115
  223.9 7.5 all-to-all-done.2
  237.6 8.5 collective-permute-done.15
  246.2 4.8 collective-permute-start.23
  254.0 4.8 collective-permute-start.24
  261.9 4.8 collective-permute-start.25
  269.7 4.8 collective-permute-start.26
  277.6 4.8 collective-permute-start.27
  285.6 5.1 collective-permute-start.28
  295.0 5.6 collective-permute-start.29
  313.7 20.3 %all_to_all.52 = bf16[8,64,384]{2,1,0:T(8,128)(2,1)S(1)} all-to-all(bf16[8,64,384]{2,1,0:T(8,128)(2,1)S(1)} %bitcast.105), channel_id=1, replica_groups=mesh['store'=8,'mp'=16] {'store'}, dimensions={0} | all-to-all | bytes 786432 | tf_op jit(solution)/shard_map/all_to_all | solution.py:86
  336.5 71.0 %reduce-scatter.15.cloned.1.call-done = f32[32,64]{1,0:T(8,128)} async-done(((f32[512,64]{1,0:T(8,128)}), f32[32,64]{1,0:T(8,128)}) %reduce-scatter.15.cloned.1.call-update) | async-done | bytes 8208 | tf_op jit(solution)/shard_map/reduce_scatter | solution.py:102
  408.2 17.2 %all_gather.21 = bf16[512,64]{1,0:T(8,128)(2,1)S(1)} all-gather(bf16[32,64]{1,0:T(8,128)(2,1)S(1)} %convert_element_type.136), channel_id=1, replica_groups=mesh['store'=8,'mp'=16] {'mp'}, dimensions={0}, use_global_device_ids=true | all-gather | bytes 69632 | tf_op jit(solution)/shard_map/all_gather | solution.py:105
  427.2 20.9 %all_to_all.53 = bf16[8,64,384]{2,1,0:T(8,128)(2,1)S(1)} all-to-all(bf16[8,64,384]{2,1,0:T(8,128)(2,1)S(1)} %bitcast.114), channel_id=1, replica_groups=mesh['store'=8,'mp'=16] {'store'}, dimensions={0} | all-to-all | bytes 786432 | tf_op jit(solution)/shard_map/all_to_all | solution.py:115
  454.3 8.9 collective-permute-done.30
  471.1 4.8 collective-permute-start.39
  478.9 4.8 collective-permute-start.40
  486.8 4.8 collective-permute-start.41
  494.6 4.8 collective-permute-start.42
  502.4 5.0 collective-permute-start.43
  511.3 5.4 collective-permute-start.44
  530.5 19.9 %all_to_all.54 = bf16[8,64,384]{2,1,0:T(8,128)(2,1)S(1)} all-to-all(bf16[8,64,384]{2,1,0:T(8,128)(2,1)S(1)} %bitcast.106), channel_id=1, replica_groups=mesh['store'=8,'mp'=16] {'store'}, dimensions={0} | all-to-all | bytes 786432 | tf_op jit(solution)/shard_map/all_to_all | solution.py:86
  553.0 70.6 %reduce-scatter.17.cloned.1.call-done = f32[32,64]{1,0:T(8,128)} async-done(((f32[512,64]{1,0:T(8,128)}), f32[32,64]{1,0:T(8,128)}) %reduce-scatter.17.cloned.1.call-update) | async-done | bytes 8208 | tf_op jit(solution)/shard_map/reduce_scatter | solution.py:102
  624.3 17.0 %all_gather.22 = bf16[512,64]{1,0:T(8,128)(2,1)S(1)} all-gather(bf16[32,64]{1,0:T(8,128)(2,1)S(1)} %convert_element_type.143), channel_id=1, replica_groups=mesh['store'=8,'mp'=16] {'mp'}, dimensions={0}, use_global_device_ids=true | all-gather | bytes 69632 | tf_op jit(solution)/shard_map/all_gather | solution.py:105
  643.1 21.1 %all_to_all.55 = bf16[8,64,384]{2,1,0:T(8,128)(2,1)S(1)} all-to-all(bf16[8,64,384]{2,1,0:T(8,128)(2,1)S(1)} %bitcast.116), channel_id=1, replica_groups=mesh['store'=8,'mp'=16] {'store'}, dimensions={0} | all-to-all | bytes 786432 | tf_op jit(solution)/shard_map/all_to_all | solution.py:115
  670.5 8.9 collective-permute-done.45
  687.2 4.8 collective-permute-start.54
  695.1 4.8 collective-permute-start.55
  702.9 4.8 collective-permute-start.56
  710.8 4.8 collective-permute-start.57
  718.6 5.0 collective-permute-start.58
  727.5 5.4 collective-permute-start.59
  746.6 19.9 %all_to_all.56 = bf16[8,64,384]{2,1,0:T(8,128)(2,1)S(1)} all-to-all(bf16[8,64,384]{2,1,0:T(8,128)(2,1)S(1)} %bitcast.104), channel_id=1, replica_groups=mesh['store'=8,'mp'=16] {'store'}, dimensions={0} | all-to-all | bytes 786432 | tf_op jit(solution)/shard_map/all_to_all | solution.py:86
  769.1 70.6 %reduce-scatter.19.cloned.1.call-done = f32[32,64]{1,0:T(8,128)} async-done(((f32[512,64]{1,0:T(8,128)}), f32[32,64]{1,0:T(8,128)}) %reduce-scatter.19.cloned.1.call-update) | async-done | bytes 8208 | tf_op jit(solution)/shard_map/reduce_scatter | solution.py:102
  840.4 17.0 %all_gather.23 = bf16[512,64]{1,0:T(8,128)(2,1)S(1)} all-gather(bf16[32,64]{1,0:T(8,128)(2,1)S(1)} %convert_element_type.150), channel_id=1, replica_groups=mesh['store'=8,'mp'=16] {'mp'}, dimensions={0}, use_global_device_ids=true | all-gather | bytes 69632 | tf_op jit(solution)/shard_map/all_gather | solution.py:105
  859.2 20.9 %all_to_all.57 = bf16[8,64,384]{2,1,0:T(8,128)(2,1)S(1)} all-to-all(bf16[8,64,384]{2,1,0:T(8,128)(2,1)S(1)} %bitcast.112), channel_id=1, replica_groups=mesh['store'=8,'mp'=16] {'store'}, dimensions={0} | all-to-all | bytes 786432 | tf_op jit(solution)/shard_map/all_to_all | solution.py:115
  881.9 5.0 fusion.28
  (265 shorter events, 204.7 us)
Async XLA Ops:
  6.5 100.6 %all-gather.3.cloned.1.call-start = ((), (), s32[]{:S(2)}) async-start(), calls=%async_computation.13 | async-start | bytes 3538944 | tf_op jit(solution)/shard_map/all_gather | solution.py:25
  8.7 110.3 %all-gather.5.cloned.1.call-start = ((), (), s32[]{:S(2)}) async-start(), calls=%async_computation.14 | async-start | bytes 3538944 | tf_op jit(solution)/shard_map/all_gather | solution.py:26
  8.7 10.6 %collective-permute-start = (bf16[256,384]{1,0:T(8,128)(2,1)}, bf16[256,384]{1,0:T(8,128)(2,1)S(1)}, u32[]{:S(2)}, u32[]{:S(2)}) collective-permute-start(bf16[256,384]{1,0:T(8,128)(2,1)} %param.10), channel_id=1, source_target_pairs={{0,1},{1,2},{2,3},{3,4},{4,5},{5,6},{6,7},{7,8},{8,9},{9,10},{10,1... | collective-permute-start | bytes 589832 | tf_op jit(solution)/shard_map/ppermute | solution.py:73
  19.3 8.5 collective-permute-start.1
  19.3 10.6 %collective-permute-start.8 = (bf16[256,384]{1,0:T(8,128)(2,1)}, bf16[256,384]{1,0:T(8,128)(2,1)S(1)}, u32[]{:S(2)}, u32[]{:S(2)}) collective-permute-start(bf16[256,384]{1,0:T(8,128)(2,1)} %param.10), channel_id=1, source_target_pairs={{0,15},{1,0},{2,1},{3,2},{4,3},{5,4},{6,5},{7,6},{8,7},{9,8},{10,9... | collective-permute-start | bytes 589832 | tf_op jit(solution)/shard_map/ppermute | solution.py:75
  37.4 7.8 collective-permute-start.10
  43.5 7.8 collective-permute-start.4
  45.2 19.9 %collective-permute-start.11 = (bf16[256,384]{1,0:T(8,128)(2,1)S(1)}, bf16[256,384]{1,0:T(8,128)(2,1)S(1)}, u32[]{:S(2)}, u32[]{:S(2)}) collective-permute-start(bf16[256,384]{1,0:T(8,128)(2,1)S(1)} %collective-permute-done.10), channel_id=1, source_target_pairs={{0,15},{1,0},{2,1},{3,2},{4,3},{5,4},{6,5},{7,6},{8,7},{9,8},{10,9... | collective-permute-start | bytes 589832 | tf_op jit(solution)/shard_map/ppermute | solution.py:75
  51.3 18.8 %collective-permute-start.5 = (bf16[256,384]{1,0:T(8,128)(2,1)S(1)}, bf16[256,384]{1,0:T(8,128)(2,1)S(1)}, u32[]{:S(2)}, u32[]{:S(2)}) collective-permute-start(bf16[256,384]{1,0:T(8,128)(2,1)S(1)} %collective-permute-done.4), channel_id=1, source_target_pairs={{0,1},{1,2},{2,3},{3,4},{4,5},{5,6},{6,7},{7,8},{8,9},{9,10},{10,1... | collective-permute-start | bytes 589832 | tf_op jit(solution)/shard_map/ppermute | solution.py:73
  54.3 18.6 %all-to-all-start = ((s32[8,1,64]{2,1,0:T(1,128)}), s32[8,1,64]{2,1,0:T(1,128)S(1)}, u32[]{:S(2)}, u32[]{:S(2)}) async-start(s32[8,1,64]{2,1,0:T(1,128)} %all_to_all.33), calls=%async_computation | async-start | bytes 8192 | tf_op jit(solution)/shard_map/all_to_all | solution.py:87
  65.0 9.2 %collective-permute-start.12 = (bf16[256,384]{1,0:T(8,128)(2,1)S(1)}, bf16[256,384]{1,0:T(8,128)(2,1)S(1)}, u32[]{:S(2)}, u32[]{:S(2)}) collective-permute-start(bf16[256,384]{1,0:T(8,128)(2,1)S(1)} %collective-permute-done.11), channel_id=1, source_target_pairs={{0,15},{1,0},{2,1},{3,2},{4,3},{5,4},{6,5},{7,6},{8,7},{9,8},{10,9... | collective-permute-start | bytes 589832 | tf_op jit(solution)/shard_map/ppermute | solution.py:75
  70.1 9.7 %collective-permute-start.6 = (bf16[256,384]{1,0:T(8,128)(2,1)S(1)}, bf16[256,384]{1,0:T(8,128)(2,1)S(1)}, u32[]{:S(2)}, u32[]{:S(2)}) collective-permute-start(bf16[256,384]{1,0:T(8,128)(2,1)S(1)} %collective-permute-done.5), channel_id=1, source_target_pairs={{0,1},{1,2},{2,3},{3,4},{4,5},{5,6},{6,7},{7,8},{8,9},{9,10},{10,1... | collective-permute-start | bytes 589832 | tf_op jit(solution)/shard_map/ppermute | solution.py:73
  74.3 8.8 collective-permute-start.13
  79.8 9.0 %collective-permute-start.7 = (bf16[256,384]{1,0:T(8,128)(2,1)S(1)}, bf16[256,384]{1,0:T(8,128)(2,1)S(1)}, u32[]{:S(2)}, u32[]{:S(2)}) collective-permute-start(bf16[256,384]{1,0:T(8,128)(2,1)S(1)} %collective-permute-done.6), channel_id=1, source_target_pairs={{0,1},{1,2},{2,3},{3,4},{4,5},{5,6},{6,7},{7,8},{8,9},{9,10},{10,1... | collective-permute-start | bytes 589832 | tf_op jit(solution)/shard_map/ppermute | solution.py:73
  83.1 8.3 collective-permute-start.14
  100.4 14.4 %all-to-all-start.1 = ((bf16[8,64,384]{2,1,0:T(8,128)(2,1)}), bf16[8,64,384]{2,1,0:T(8,128)(2,1)S(1)}, u32[]{:S(2)}, u32[]{:S(2)}) async-start(bf16[8,64,384]{2,1,0:T(8,128)(2,1)} %bitcast.6), calls=%async_computation.1 | async-start | bytes 786432 | tf_op jit(solution)/shard_map/all_to_all | solution.py:86
  107.1 83.3 %reduce-scatter.13.cloned.1.call-start = ((), (), s32[]{:S(2)}) async-start(), calls=%async_computation.15 | async-start | bytes 278528 | tf_op jit(solution)/shard_map/reduce_scatter | solution.py:102
  210.8 20.6 %all-to-all-start.2 = ((bf16[8,64,384]{2,1,0:T(8,128)(2,1)}), bf16[8,64,384]{2,1,0:T(8,128)(2,1)S(1)}, u32[]{:S(2)}, u32[]{:S(2)}) async-start(bf16[8,64,384]{2,1,0:T(8,128)(2,1)} %bitcast.110), calls=%async_computation.2 | async-start | bytes 786432 | tf_op jit(solution)/shard_map/all_to_all | solution.py:115
  223.7 183.8 %reduce-scatter.15.cloned.1.call-start = ((), (), s32[]{:S(2)}) async-start(), calls=%async_computation.16 | async-start | bytes 278528 | tf_op jit(solution)/shard_map/reduce_scatter | solution.py:102
  237.5 8.6 collective-permute-start.15
  246.2 7.8 collective-permute-start.23
  254.0 7.8 collective-permute-start.17
  254.0 7.8 collective-permute-start.24
  269.7 7.8 collective-permute-start.26
  277.5 8.1 collective-permute-start.20
  277.6 8.1 collective-permute-start.27
  285.6 9.2 %collective-permute-start.21 = (bf16[256,384]{1,0:T(8,128)(2,1)S(1)}, bf16[256,384]{1,0:T(8,128)(2,1)S(1)}, u32[]{:S(2)}, u32[]{:S(2)}) collective-permute-start(bf16[256,384]{1,0:T(8,128)(2,1)S(1)} %collective-permute-done.20), channel_id=1, source_target_pairs={{0,1},{1,2},{2,3},{3,4},{4,5},{5,6},{6,7},{7,8},{8,9},{9,10},{10,1... | collective-permute-start | bytes 589832 | tf_op jit(solution)/shard_map/ppermute | solution.py:73
  285.6 9.4 %collective-permute-start.28 = (bf16[256,384]{1,0:T(8,128)(2,1)S(1)}, bf16[256,384]{1,0:T(8,128)(2,1)S(1)}, u32[]{:S(2)}, u32[]{:S(2)}) collective-permute-start(bf16[256,384]{1,0:T(8,128)(2,1)S(1)} %collective-permute-done.27), channel_id=1, source_target_pairs={{0,15},{1,0},{2,1},{3,2},{4,3},{5,4},{6,5},{7,6},{8,7},{9,8},{10,9... | collective-permute-start | bytes 589832 | tf_op jit(solution)/shard_map/ppermute | solution.py:75
  294.9 9.8 %collective-permute-start.22 = (bf16[256,384]{1,0:T(8,128)(2,1)S(1)}, bf16[256,384]{1,0:T(8,128)(2,1)S(1)}, u32[]{:S(2)}, u32[]{:S(2)}) collective-permute-start(bf16[256,384]{1,0:T(8,128)(2,1)S(1)} %collective-permute-done.21), channel_id=1, source_target_pairs={{0,1},{1,2},{2,3},{3,4},{4,5},{5,6},{6,7},{7,8},{8,9},{9,10},{10,1... | collective-permute-start | bytes 589832 | tf_op jit(solution)/shard_map/ppermute | solution.py:73
  295.0 10.4 %collective-permute-start.29 = (bf16[256,384]{1,0:T(8,128)(2,1)S(1)}, bf16[256,384]{1,0:T(8,128)(2,1)S(1)}, u32[]{:S(2)}, u32[]{:S(2)}) collective-permute-start(bf16[256,384]{1,0:T(8,128)(2,1)S(1)} %collective-permute-done.28), channel_id=1, source_target_pairs={{0,15},{1,0},{2,1},{3,2},{4,3},{5,4},{6,5},{7,6},{8,7},{9,8},{10,9... | collective-permute-start | bytes 589832 | tf_op jit(solution)/shard_map/ppermute | solution.py:75
  336.5 287.1 %reduce-scatter.17.cloned.1.call-start = ((), (), s32[]{:S(2)}) async-start(), calls=%async_computation.17 | async-start | bytes 278528 | tf_op jit(solution)/shard_map/reduce_scatter | solution.py:102
  454.2 9.0 %collective-permute-start.30 = (bf16[256,384]{1,0:T(8,128)(2,1)S(1)}, bf16[256,384]{1,0:T(8,128)(2,1)S(1)}, u32[]{:S(2)}, u32[]{:S(2)}) collective-permute-start(bf16[256,384]{1,0:T(8,128)(2,1)S(1)} %fusion.30), channel_id=1, source_target_pairs={{0,1},{1,2},{2,3},{3,4},{4,5},{5,6},{6,7},{7,8},{8,9},{9,10},{10,1... | collective-permute-start | bytes 589832 | tf_op jit(solution)/shard_map/ppermute | solution.py:73
  463.2 7.8 collective-permute-start.31
  463.2 7.8 collective-permute-start.38
  478.9 7.8 collective-permute-start.40
  486.7 7.8 collective-permute-start.34
  502.4 8.9 collective-permute-start.36
  502.4 8.9 collective-permute-start.43
  511.3 10.2 %collective-permute-start.37 = (bf16[256,384]{1,0:T(8,128)(2,1)S(1)}, bf16[256,384]{1,0:T(8,128)(2,1)S(1)}, u32[]{:S(2)}, u32[]{:S(2)}) collective-permute-start(bf16[256,384]{1,0:T(8,128)(2,1)S(1)} %collective-permute-done.36), channel_id=1, source_target_pairs={{0,1},{1,2},{2,3},{3,4},{4,5},{5,6},{6,7},{7,8},{8,9},{9,10},{10,1... | collective-permute-start | bytes 589832 | tf_op jit(solution)/shard_map/ppermute | solution.py:73
  511.3 10.8 %collective-permute-start.44 = (bf16[256,384]{1,0:T(8,128)(2,1)S(1)}, bf16[256,384]{1,0:T(8,128)(2,1)S(1)}, u32[]{:S(2)}, u32[]{:S(2)}) collective-permute-start(bf16[256,384]{1,0:T(8,128)(2,1)S(1)} %collective-permute-done.43), channel_id=1, source_target_pairs={{0,15},{1,0},{2,1},{3,2},{4,3},{5,4},{6,5},{7,6},{8,7},{9,8},{10,9... | collective-permute-start | bytes 589832 | tf_op jit(solution)/shard_map/ppermute | solution.py:75
  552.9 286.8 %reduce-scatter.19.cloned.1.call-start = ((), (), s32[]{:S(2)}) async-start(), calls=%async_computation.18 | async-start | bytes 278528 | tf_op jit(solution)/shard_map/reduce_scatter | solution.py:102
  670.4 9.0 %collective-permute-start.45 = (bf16[256,384]{1,0:T(8,128)(2,1)S(1)}, bf16[256,384]{1,0:T(8,128)(2,1)S(1)}, u32[]{:S(2)}, u32[]{:S(2)}) collective-permute-start(bf16[256,384]{1,0:T(8,128)(2,1)S(1)} %fusion.29), channel_id=1, source_target_pairs={{0,1},{1,2},{2,3},{3,4},{4,5},{5,6},{6,7},{7,8},{8,9},{9,10},{10,1... | collective-permute-start | bytes 589832 | tf_op jit(solution)/shard_map/ppermute | solution.py:73
  679.4 7.8 collective-permute-start.53
  687.2 7.8 collective-permute-start.47
  718.6 8.9 collective-permute-start.51
  718.6 8.9 collective-permute-start.58
  727.5 10.1 %collective-permute-start.52 = (bf16[256,384]{1,0:T(8,128)(2,1)S(1)}, bf16[256,384]{1,0:T(8,128)(2,1)S(1)}, u32[]{:S(2)}, u32[]{:S(2)}) collective-permute-start(bf16[256,384]{1,0:T(8,128)(2,1)S(1)} %collective-permute-done.51), channel_id=1, source_target_pairs={{0,1},{1,2},{2,3},{3,4},{4,5},{5,6},{6,7},{7,8},{8,9},{9,10},{10,1... | collective-permute-start | bytes 589832 | tf_op jit(solution)/shard_map/ppermute | solution.py:73
  727.5 10.8 %collective-permute-start.59 = (bf16[256,384]{1,0:T(8,128)(2,1)S(1)}, bf16[256,384]{1,0:T(8,128)(2,1)S(1)}, u32[]{:S(2)}, u32[]{:S(2)}) collective-permute-start(bf16[256,384]{1,0:T(8,128)(2,1)S(1)} %collective-permute-done.58), channel_id=1, source_target_pairs={{0,15},{1,0},{2,1},{3,2},{4,3},{5,4},{6,5},{7,6},{8,7},{9,8},{10,9... | collective-permute-start | bytes 589832 | tf_op jit(solution)/shard_map/ppermute | solution.py:75
  (35 other events, 961.8 us)
Sparse Core Ops, SparseCore 0:
  9.0 31.4 all-gather.2
  42.2 27.6 all-gather.4
  119.0 71.2 reduce-scatter.12
  336.6 70.8 reduce-scatter.14
  553.0 70.5 reduce-scatter.16
  769.2 70.4 reduce-scatter.18
